TPU v7x, 512 devices: a whole 4x4x16 slice. The times are simulated.
512 devices in a mesh: rep: 2 (over core), row: 16 (over y, x), col: 16 (over z).
Axes of the slice: x: 4, y: 4, z: 16, core: 2. Of those that a mesh axis runs over, the one named last changes fastest.
Arguments:
- residual: bfloat16 [16384, 2048], P(('rep', 'row'), 'col'), may hold values from -6 to 6
- post_gain: float32 [2048], replicated, may hold values from 0.25 to 1.75
- w_gate: bfloat16 [2048, 6144], P('row', 'col'), may hold values from -0.125 to 0.125
- w_up: bfloat16 [2048, 6144], P('row', 'col'), may hold values from -0.125 to 0.125
- w_down: bfloat16 [6144, 2048], P('col', 'row'), may hold values from -0.078125 to 0.078125
- next_gain: float32 [2048], replicated, may hold values from 0.25 to 1.75
- w_qkv: bfloat16 [2048, 4096], P('row', 'col'), may hold values from -0.125 to 0.125
- q_gain: float32 [128], replicated, may hold values from 0.25 to 1.75
- k_gain: float32 [128], replicated, may hold values from 0.25 to 1.75
- source: int32 [16384], P(('rep', 'row')), may hold values from 0 to 16383, as said below
Outputs:
- moved_residual: bfloat16 [16384, 2048], P(('rep', 'row'), 'col')
- moved_qkv: bfloat16 [16384, 4096], P(('rep', 'row'), 'col')
Inputs may be any that keep to these rules, and one draw needn't show every extreme that they name: source is a permutation of all rows. Rows are grouped in blocks of 512 (block b holds rows b * 512 to (b + 1) * 512 - 1, blocks of replica 0 first); output block b takes its rows from input block b or from the block of the same row index in the other replica, at most 128 of them from the other replica, and some block takes exactly 128. A block takes as many rows from the other replica as it gives to it.
All inputs are finite; a program needn't handle non-finite values.
Results may differ from a plain program's by a relative error of at most 0.0065.
Values may be sent and summed in bfloat16 or wider, within the bound.
A program may use at most 64 MiB of HBM per device.

v0:
```python
import jax
import jax.numpy as jnp
from jax import lax
from jax.sharding import PartitionSpec as P

HEADS = 16
KV_HEADS = 8
HD = 128
epsilon = 1e-06


def swapped(x, axis, apart):
    return lax.ppermute(x, axis, [(i, i ^ 1 << apart) for i in range(lax.axis_size(axis))])


def normalize(values, gain):
    scale = lax.rsqrt(jnp.mean(values * values, axis=-1, keepdims=True) + epsilon)
    return values * scale * gain


def per_device(residual, post_gain, w_gate, w_up, w_down, next_gain, w_qkv, q_gain, k_gain, source):
    tok_rows = residual.shape[0]
    col_index = lax.axis_index("col")
    gathered = lax.all_gather(residual, "col", axis=1, tiled=True)
    stream = gathered.astype(jnp.float32)
    normed = normalize(stream, post_gain).astype(jnp.bfloat16)
    columns = normed
    gate_proj = jnp.dot(
        columns,
        lax.all_gather(w_gate, "row", axis=0, tiled=True),
        preferred_element_type=jnp.float32,
    )
    up_proj = jnp.dot(
        columns, lax.all_gather(w_up, "row", axis=0, tiled=True), preferred_element_type=jnp.float32
    )
    hidden = (jax.nn.silu(gate_proj) * up_proj).astype(jnp.bfloat16)
    partial_value = jnp.dot(
        hidden,
        lax.all_gather(w_down, "row", axis=1, tiled=True),
        preferred_element_type=jnp.float32,
    )
    mlp_share = lax.psum_scatter(partial_value, "col", scatter_dimension=1, tiled=True)
    resid_own = (residual.astype(jnp.float32) + mlp_share).astype(jnp.bfloat16)
    resid_full = lax.all_gather(resid_own, "col", axis=1, tiled=True)
    next_normed = normalize(resid_full.astype(jnp.float32), next_gain).astype(jnp.bfloat16)
    proj_width = w_qkv.shape[1]
    columns = next_normed
    projected = jnp.dot(
        columns,
        lax.all_gather(w_qkv, "row", axis=0, tiled=True),
        preferred_element_type=jnp.float32,
    )
    head_count = proj_width // HD
    per_head = projected.reshape(tok_rows, head_count, HD)
    head_number = col_index * head_count + jnp.arange(head_count, dtype=jnp.int32)
    is_query = head_number < HEADS
    is_key = jnp.logical_and(head_number >= HEADS, head_number < HEADS + KV_HEADS)
    head_gain = jnp.where(is_query[:, None], q_gain[None, :], k_gain[None, :])
    head_scaled = normalize(per_head, head_gain)
    keep_norm = jnp.logical_or(is_query, is_key)[None, :, None]
    qkv_own = (
        jnp.where(keep_norm, head_scaled, per_head)
        .reshape(tok_rows, proj_width)
        .astype(jnp.bfloat16)
    )
    my_block = lax.axis_index("rep") * lax.axis_size("row") + lax.axis_index("row")
    from_peer = source // tok_rows != my_block
    local_row = source % tok_rows
    peer_resid, peer_qkv = swapped((resid_own, qkv_own), "rep", 0)
    picked = local_row + tok_rows * from_peer.astype(jnp.int32)
    moved_residual = jnp.take(jnp.concatenate([resid_own, peer_resid], axis=0), picked, axis=0)
    moved_qkv = jnp.take(jnp.concatenate([qkv_own, peer_qkv], axis=0), picked, axis=0)
    return (moved_residual, moved_qkv)


def solution(mesh):
    return jax.shard_map(
        per_device,
        mesh=mesh,
        in_specs=(
            P(("rep", "row"), "col"),
            P(),
            P("row", "col"),
            P("row", "col"),
            P("col", "row"),
            P(),
            P("row", "col"),
            P(),
            P(),
            P(("rep", "row")),
        ),
        out_specs=(P(("rep", "row"), "col"), P(("rep", "row"), "col")),
        check_vma=False,
    )
```

profile of v0, /device:TPU:1, one launch (start us, length us, event | category | flops | bytes accessed | tf_op | source)
XLA Modules:
  0.0 517.1 jit_solution(11629037548047053310)
XLA Ops:
  7.2 0.0 copy-start.7
  7.2 0.0 all-gather.7.cloned.1.call-start
  7.2 0.7 all-gather.7.cloned.1.call-update
  7.9 0.0 all-gather.9.cloned.1.call-start
  8.0 0.7 all-gather.9.cloned.1.call-update
  8.7 0.0 all-gather.11.cloned.1.call-start
  8.7 0.7 all-gather.11.cloned.1.call-update
  9.4 0.0 all-gather.13.cloned.1.call-start
  9.4 0.5 all-gather.13.cloned.1.call-update
  10.0 0.0 reduce-scatter.2.cloned.1.call-start
  10.0 74.2 %all-gather.7.cloned.1.call-done = bf16[512,2048]{1,0:T(8,128)(2,1)} async-done(((bf16[512,128]{1,0:T(8,128)(2,1)}), bf16[512,2048]{1,0:T(8,128)(2,1)}) %all-gather.7.cloned.1.call-update) | async-done | bytes 2097168 | tf_op jit(solution)/shard_map/all_gather | solution.py:24
  84.2 2.2 fusion
  86.4 65.4 %all-gather.9.cloned.1.call-done = bf16[2048,384]{1,0:T(8,128)(2,1)} async-done(((bf16[128,384]{1,0:T(8,128)(2,1)}), bf16[2048,384]{1,0:T(8,128)(2,1)}) %all-gather.9.cloned.1.call-update) | async-done | bytes 1572880 | tf_op jit(solution)/shard_map/all_gather | solution.py:30
  151.8 0.0 copy-done.7
  151.8 0.0 copy-done.1
  151.8 2.7 fusion.19
  154.5 59.1 %all-gather.11.cloned.1.call-done = bf16[2048,384]{1,0:T(8,128)(2,1)} async-done(((bf16[128,384]{1,0:T(8,128)(2,1)}), bf16[2048,384]{1,0:T(8,128)(2,1)}) %all-gather.11.cloned.1.call-update) | async-done | bytes 1572880 | tf_op jit(solution)/shard_map/all_gather | solution.py:34
  213.6 62.7 %all-gather.13.cloned.1.call-done = bf16[384,2048]{1,0:T(8,128)(2,1)} async-done(((bf16[384,128]{1,0:T(8,128)(2,1)}), bf16[384,2048]{1,0:T(8,128)(2,1)}) %all-gather.13.cloned.1.call-update) | async-done | bytes 1572880 | tf_op jit(solution)/shard_map/all_gather | solution.py:39
  276.3 6.2 %fusion.11 = f32[512,2048]{1,0:T(8,128)} fusion(bf16[384,2048]{1,0:T(8,128)(2,1)} %all-gather.13.cloned.1.call-done, bf16[2048,384]{1,0:T(8,128)(2,1)} %all-gather.11.cloned.1.call-done, f32[512,384]{1,0:T(8,128)S(1)} %fusion.19, bf16[512,2048]{1,0:T(8,128)(2,1)S(1)} %copy-done.1, f32[2048]{0:T(1024)S(1)} %copy-done.7, f32[512]{0:T(512)S(1)} %add_rsqrt_fusion.2), kind=kOutput, calls=%fused_computation.17 | convolution fusion | flops 1615986688 | bytes 10233856 | tf_op jit(solution)/shard_map/dot_general | solution.py:37
  282.6 0.0 reduce-scatter.2.cloned.1.call-update
  282.6 0.0 copy-start.8
  282.6 0.0 all-gather.15.cloned.1.call-start
  282.6 71.0 %reduce-scatter.2.cloned.1.call-done = f32[512,128]{1,0:T(8,128)} async-done(((f32[512,2048]{1,0:T(8,128)}), f32[512,128]{1,0:T(8,128)}) %reduce-scatter.2.cloned.1.call-update) | async-done | bytes 262160 | tf_op jit(solution)/shard_map/reduce_scatter | solution.py:42
  353.6 0.0 copy-done.3
  353.6 1.6 add_convert_fusion
  355.3 0.0 all-gather.15.cloned.1.call-update
  355.3 0.0 all-gather.17.cloned.1.call-start
  355.3 0.7 all-gather.17.cloned.1.call-update
  356.1 0.0 copy-done.4
  356.1 0.1 broadcast_bitcast_fusion
  356.2 0.0 copy-done.6
  356.2 0.1 bitcast_select_fusion
  356.3 11.9 %collective-permute-start = (bf16[512,128]{1,0:T(8,128)(2,1)}, bf16[512,128]{1,0:T(8,128)(2,1)S(1)}, u32[]{:S(2)}, u32[]{:S(2)}) collective-permute-start(bf16[512,128]{1,0:T(8,128)(2,1)} %add_convert_fusion), channel_id=1, source_target_pairs={{0,256},{256,0},{1,257},{257,1},{2,258},{258,2},{3,259},{259,3},{4... | collective-permute-start | bytes 393224 | tf_op jit(solution)/shard_map/ppermute | solution.py:13
  368.2 64.5 %all-gather.15.cloned.1.call-done = bf16[512,2048]{1,0:T(8,128)(2,1)} async-done(((bf16[512,128]{1,0:T(8,128)(2,1)}), bf16[512,2048]{1,0:T(8,128)(2,1)}) %all-gather.15.cloned.1.call-update) | async-done | bytes 2097168 | tf_op jit(solution)/shard_map/all_gather | solution.py:44
  432.6 2.2 fusion.3
  434.9 0.0 copy-start.2
  434.9 63.7 %all-gather.17.cloned.1.call-done = bf16[2048,256]{1,0:T(8,128)(2,1)} async-done(((bf16[128,256]{1,0:T(8,128)(2,1)}), bf16[2048,256]{1,0:T(8,128)(2,1)}) %all-gather.17.cloned.1.call-update) | async-done | bytes 1048592 | tf_op jit(solution)/shard_map/all_gather | solution.py:50
  498.6 2.2 bitcast_reduce_fusion
  500.8 0.1 fusion.23
  500.9 4.0 collective-permute-start.1
  504.9 0.0 collective-permute-done
  505.0 1.3 gather_fusion
  506.3 0.8 broadcast_select_fusion.1
  507.1 0.0 collective-permute-done.1
  507.1 0.1 pad_maximum_fusion
  507.2 0.2 copy.13
  507.4 2.0 gather_fusion.1
  509.4 0.8 broadcast_select_fusion
  (17 shorter events, 0.1 us)
Async XLA Ops:
  7.2 144.7 %copy-start.7 = (f32[2048]{0:T(1024)S(1)}, f32[2048]{0:T(1024)}, u32[]{:S(2)}) copy-start(f32[2048]{0:T(1024)} %param.11) | copy-start | bytes 24580
  7.2 77.0 %all-gather.7.cloned.1.call-start = ((), (), s32[]{:S(2)}) async-start(), calls=%async_computation.1 | async-start | bytes 2228224 | tf_op jit(solution)/shard_map/all_gather | solution.py:24
  7.9 143.9 %all-gather.9.cloned.1.call-start = ((), (), s32[]{:S(2)}) async-start(), calls=%async_computation.2 | async-start | bytes 1671168 | tf_op jit(solution)/shard_map/all_gather | solution.py:30
  8.7 204.9 %all-gather.11.cloned.1.call-start = ((), (), s32[]{:S(2)}) async-start(), calls=%async_computation.3 | async-start | bytes 1671168 | tf_op jit(solution)/shard_map/all_gather | solution.py:34
  9.4 266.9 %all-gather.13.cloned.1.call-start = ((), (), s32[]{:S(2)}) async-start(), calls=%async_computation.4 | async-start | bytes 1671168 | tf_op jit(solution)/shard_map/all_gather | solution.py:39
  10.0 343.7 %reduce-scatter.2.cloned.1.call-start = ((), (), s32[]{:S(2)}) async-start(), calls=%async_computation.5 | async-start | bytes 4456448 | tf_op jit(solution)/shard_map/reduce_scatter | solution.py:42
  84.2 67.6 %copy-start.1 = (bf16[512,2048]{1,0:T(8,128)(2,1)S(1)}, bf16[512,2048]{1,0:T(8,128)(2,1)}, u32[]{:S(2)}) copy-start(bf16[512,2048]{1,0:T(8,128)(2,1)} %all-gather.7.cloned.1.call-done) | copy-start | bytes 6291460
  282.5 71.1 %copy-start.3 = (bf16[512,128]{1,0:T(8,128)(2,1)S(1)}, bf16[512,128]{1,0:T(8,128)(2,1)}, u32[]{:S(2)}) copy-start(bf16[512,128]{1,0:T(8,128)(2,1)} %param.10) | copy-start | bytes 393220
  282.6 73.5 %copy-start.4 = (s32[512]{0:T(512)S(1)}, s32[512]{0:T(512)}, u32[]{:S(2)}) copy-start(s32[512]{0:T(512)} %param.19) | copy-start | bytes 6148
  282.6 73.6 %copy-start.5 = (f32[128]{0:T(128)S(1)}, f32[128]{0:T(128)}, u32[]{:S(2)}) copy-start(f32[128]{0:T(128)} %param.18) | copy-start | bytes 1540
  282.6 73.6 %copy-start.6 = (f32[128]{0:T(128)S(1)}, f32[128]{0:T(128)}, u32[]{:S(2)}) copy-start(f32[128]{0:T(128)} %param.17) | copy-start | bytes 1540
  282.6 216.0 %copy-start.8 = (f32[2048]{0:T(1024)S(1)}, f32[2048]{0:T(1024)}, u32[]{:S(2)}) copy-start(f32[2048]{0:T(1024)} %param.15) | copy-start | bytes 24580
  282.6 150.0 %all-gather.15.cloned.1.call-start = ((), (), s32[]{:S(2)}) async-start(), calls=%async_computation.6 | async-start | bytes 2228224 | tf_op jit(solution)/shard_map/all_gather | solution.py:44
  355.3 143.3 %all-gather.17.cloned.1.call-start = ((), (), s32[]{:S(2)}) async-start(), calls=%async_computation.7 | async-start | bytes 1114112 | tf_op jit(solution)/shard_map/all_gather | solution.py:50
  356.3 148.7 %collective-permute-start = (bf16[512,128]{1,0:T(8,128)(2,1)}, bf16[512,128]{1,0:T(8,128)(2,1)S(1)}, u32[]{:S(2)}, u32[]{:S(2)}) collective-permute-start(bf16[512,128]{1,0:T(8,128)(2,1)} %add_convert_fusion), channel_id=1, source_target_pairs={{0,256},{256,0},{1,257},{257,1},{2,258},{258,2},{3,259},{259,3},{4... | collective-permute-start | bytes 393224 | tf_op jit(solution)/shard_map/ppermute | solution.py:13
  432.6 65.9 %copy-start = (bf16[512,2048]{1,0:T(8,128)(2,1)S(1)}, bf16[512,2048]{1,0:T(8,128)(2,1)}, u32[]{:S(2)}) copy-start(bf16[512,2048]{1,0:T(8,128)(2,1)} %all-gather.15.cloned.1.call-done) | copy-start | bytes 6291460
  434.9 70.1 %copy-start.2 = (bf16[512,128]{1,0:T(8,128)(2,1)S(1)}, bf16[512,128]{1,0:T(8,128)(2,1)}, u32[]{:S(2)}) copy-start(bf16[512,128]{1,0:T(8,128)(2,1)} %add_convert_fusion) | copy-start | bytes 393220
  500.9 6.2 %collective-permute-start.1 = (bf16[512,256]{0,1:T(8,128)(2,1)S(1)}, bf16[512,256]{0,1:T(8,128)(2,1)S(1)}, u32[]{:S(2)}, u32[]{:S(2)}) collective-permute-start(bf16[512,256]{0,1:T(8,128)(2,1)S(1)} %fusion.23), channel_id=1, source_target_pairs={{0,256},{256,0},{1,257},{257,1},{2,258},{258,2},{3,259},{259,3},{4... | collective-permute-start | bytes 786440 | tf_op jit(solution)/shard_map/ppermute | solution.py:13
Sparse Core Ops, SparseCore 0:
  10.0 74.1 all-gather.6
  87.2 64.5 all-gather.8
  154.8 58.7 all-gather.10
  216.4 59.8 all-gather.12
  282.7 70.8 reduce-scatter.1
  356.1 76.5 all-gather.14
  435.7 62.8 all-gather.16
where the time goes:
time: 517 us
  waiting for transfers between devices  464 us (90%)
  starting transfers between devices  16.2 us (3%)
  between operations  14.3 us (3%)
  matrix products  11.1 us (2%)
  other arithmetic  8.07 us (2%)
    all_gather x1, waiting for transfers between devices, per_device(): gathered = lax.all_gather(residual, 'col', axis=1, tiled=True)  74.2 us
    reduce_scatter x1, waiting for transfers between devices, per_device(): lax.psum_scatter(partial_value, 'col', scatter_dimension=1, tiled=True)  71 us
    all_gather x1, waiting for transfers between devices, per_device(): lax.all_gather(w_gate, 'row', axis=0, tiled=True)  65.4 us
    all_gather x1, waiting for transfers between devices, per_device(): resid_full = lax.all_gather(resid_own, 'col', axis=1, tiled=True)  64.5 us
    all_gather x1, waiting for transfers between devices, per_device(): lax.all_gather(w_qkv, 'row', axis=0, tiled=True)  63.7 us
    all_gather x1, waiting for transfers between devices, per_device(): lax.all_gather(w_down, 'row', axis=1, tiled=True)  62.7 us
    all_gather x1, waiting for transfers between devices, per_device(): lax.all_gather(w_up, 'row', axis=0, tiled=True)  59.1 us
    ppermute x2, starting transfers between devices, swapped(): lax.ppermute(x, axis, [(i, i ^ 1 << apart) for i in range(lax.axis_size(a...  15.9 us
  transfers between devices with their start and end apart: 9, of which 7 were waited for; matrix products, arithmetic and copies ran while one was open for 2% of the time, Pallas kernels for 0%

commit v1 on v0

--- a/solution.py
+++ b/solution.py
@@ -21,7 +21,12 @@
 def per_device(residual, post_gain, w_gate, w_up, w_down, next_gain, w_qkv, q_gain, k_gain, source):
     tok_rows = residual.shape[0]
     col_index = lax.axis_index("col")
-    gathered = lax.all_gather(residual, "col", axis=1, tiled=True)
+    ring = [residual]
+    for hop in range(15):
+        ring.append(lax.ppermute(ring[-1], "col", [(dev, (dev + 1) % 16) for dev in range(16)]))
+    gathered = jnp.roll(
+        jnp.concatenate(ring[::-1], axis=1), (lax.axis_index("col") + 1) * ring[0].shape[1], axis=1
+    )
     stream = gathered.astype(jnp.float32)
     normed = normalize(stream, post_gain).astype(jnp.bfloat16)
     columns = normed

time: 517 us -> 442 us (0.85)
  waiting for transfers between devices: 464 us -> 352 us
  starting transfers between devices: 16.2 us -> 47.7 us
    ppermute x0 -> x15, waiting for transfers between devices: none -> 85.2 us  [per_device(): lax.ppermute(ring[-1], 'col', [(dev, (dev + 1) % 16) for dev in range(16)])]
    all_gather x1 -> x0, waiting for transfers between devices: 74.2 us -> none  [per_device(): gathered = lax.all_gather(residual, 'col', axis=1, tiled=True)]
    all_gather x1, waiting for transfers between devices: 65.4 us -> 0.02 us  [per_device(): lax.all_gather(w_gate, 'row', axis=0, tiled=True)]
    all_gather x1, waiting for transfers between devices: 62.7 us -> 4.87 us  [per_device(): lax.all_gather(w_down, 'row', axis=1, tiled=True)]
    ppermute x0 -> x15, starting transfers between devices: none -> 31.1 us  [per_device(): lax.ppermute(ring[-1], 'col', [(dev, (dev + 1) % 16) for dev in range(16)])]
  transfers between devices with their start and end apart: 9 -> 23, of which waited for: 7 -> 20; matrix products, arithmetic and copies ran while one was open for 2% -> 3% of each run, Pallas kernels for 0% -> 0%
where the time goes in v1:
time: 442 us; the launch traced here: 441 us
  waiting for transfers between devices  352 us (80%)
  starting transfers between devices  47.7 us (11%)
  between operations  14.7 us (3%)
  matrix products  13.2 us (3%)
  local copies, waits for them, and re-layouts  6.8 us (2%)
  other arithmetic  6.18 us (1%)
    ppermute x15, waiting for transfers between devices, per_device(): lax.ppermute(ring[-1], 'col', [(dev, (dev + 1) % 16) for dev in range(16)])  85.2 us
    reduce_scatter x1, waiting for transfers between devices, per_device(): lax.psum_scatter(partial_value, 'col', scatter_dimension=1, tiled=True)  70.7 us
    all_gather x1, waiting for transfers between devices, per_device(): resid_full = lax.all_gather(resid_own, 'col', axis=1, tiled=True)  64 us
    all_gather x1, waiting for transfers between devices, per_device(): lax.all_gather(w_qkv, 'row', axis=0, tiled=True)  63.7 us
    all_gather x1, waiting for transfers between devices, per_device(): lax.all_gather(w_up, 'row', axis=0, tiled=True)  62.1 us
    ppermute x15, starting transfers between devices, per_device(): lax.ppermute(ring[-1], 'col', [(dev, (dev + 1) % 16) for dev in range(16)])  31.1 us
    ppermute x2, starting transfers between devices, swapped(): lax.ppermute(x, axis, [(i, i ^ 1 << apart) for i in range(lax.axis_size(a...  16.3 us
  transfers between devices with their start and end apart: 23, of which 20 were waited for; matrix products, arithmetic and copies ran while one was open for 3% of the time, Pallas kernels for 0%

profile of v1, /device:TPU:1, one launch (start us, length us, event | category | flops | bytes accessed | tf_op | source)
XLA Modules:
  0.0 441.0 jit_solution(10084019010184973656)
XLA Ops:
  8.0 0.7 all-gather.10.cloned.1.call-update
  8.7 4.4 collective-permute-start
  13.1 11.0 %collective-permute-done = bf16[512,128]{1,0:T(8,128)(2,1)S(1)} collective-permute-done((bf16[512,128]{1,0:T(8,128)(2,1)}, bf16[512,128]{1,0:T(8,128)(2,1)S(1)}, u32[]{:S(2)}, u32[]{:S(2)}) %collective-permute-start) | collective-permute-done | bytes 131104 | tf_op jit(solution)/shard_map/ppermute | solution.py:26
  24.1 1.9 collective-permute-start.1
  26.0 5.0 %collective-permute-done.1 = bf16[512,128]{1,0:T(8,128)(2,1)S(1)} collective-permute-done((bf16[512,128]{1,0:T(8,128)(2,1)S(1)}, bf16[512,128]{1,0:T(8,128)(2,1)S(1)}, u32[]{:S(2)}, u32[]{:S(2)}) %collective-permute-start.1) | collective-permute-done | bytes 131104 | tf_op jit(solution)/shard_map/ppermute | solution.py:26
  31.0 1.9 collective-permute-start.2
  32.9 5.0 %collective-permute-done.2 = bf16[512,128]{1,0:T(8,128)(2,1)S(1)} collective-permute-done((bf16[512,128]{1,0:T(8,128)(2,1)S(1)}, bf16[512,128]{1,0:T(8,128)(2,1)S(1)}, u32[]{:S(2)}, u32[]{:S(2)}) %collective-permute-start.2) | collective-permute-done | bytes 131104 | tf_op jit(solution)/shard_map/ppermute | solution.py:26
  37.9 1.9 collective-permute-start.3
  39.8 5.0 %collective-permute-done.3 = bf16[512,128]{1,0:T(8,128)(2,1)S(1)} collective-permute-done((bf16[512,128]{1,0:T(8,128)(2,1)S(1)}, bf16[512,128]{1,0:T(8,128)(2,1)S(1)}, u32[]{:S(2)}, u32[]{:S(2)}) %collective-permute-start.3) | collective-permute-done | bytes 131104 | tf_op jit(solution)/shard_map/ppermute | solution.py:26
  44.8 1.9 collective-permute-start.4
  46.7 5.0 %collective-permute-done.4 = bf16[512,128]{1,0:T(8,128)(2,1)S(1)} collective-permute-done((bf16[512,128]{1,0:T(8,128)(2,1)S(1)}, bf16[512,128]{1,0:T(8,128)(2,1)S(1)}, u32[]{:S(2)}, u32[]{:S(2)}) %collective-permute-start.4) | collective-permute-done | bytes 131104 | tf_op jit(solution)/shard_map/ppermute | solution.py:26
  51.7 1.9 collective-permute-start.5
  53.6 5.0 %collective-permute-done.5 = bf16[512,128]{1,0:T(8,128)(2,1)S(1)} collective-permute-done((bf16[512,128]{1,0:T(8,128)(2,1)S(1)}, bf16[512,128]{1,0:T(8,128)(2,1)S(1)}, u32[]{:S(2)}, u32[]{:S(2)}) %collective-permute-start.5) | collective-permute-done | bytes 131104 | tf_op jit(solution)/shard_map/ppermute | solution.py:26
  58.6 1.9 collective-permute-start.6
  60.6 6.2 %collective-permute-done.6 = bf16[512,128]{1,0:T(8,128)(2,1)S(1)} collective-permute-done((bf16[512,128]{1,0:T(8,128)(2,1)S(1)}, bf16[512,128]{1,0:T(8,128)(2,1)S(1)}, u32[]{:S(2)}, u32[]{:S(2)}) %collective-permute-start.6) | collective-permute-done | bytes 131104 | tf_op jit(solution)/shard_map/ppermute | solution.py:26
  66.7 1.9 collective-permute-start.7
  68.6 6.5 %collective-permute-done.7 = bf16[512,128]{1,0:T(8,128)(2,1)S(1)} collective-permute-done((bf16[512,128]{1,0:T(8,128)(2,1)S(1)}, bf16[512,128]{1,0:T(8,128)(2,1)S(1)}, u32[]{:S(2)}, u32[]{:S(2)}) %collective-permute-start.7) | collective-permute-done | bytes 131104 | tf_op jit(solution)/shard_map/ppermute | solution.py:26
  75.2 1.9 collective-permute-start.8
  77.1 5.7 %collective-permute-done.8 = bf16[512,128]{1,0:T(8,128)(2,1)S(1)} collective-permute-done((bf16[512,128]{1,0:T(8,128)(2,1)S(1)}, bf16[512,128]{1,0:T(8,128)(2,1)S(1)}, u32[]{:S(2)}, u32[]{:S(2)}) %collective-permute-start.8) | collective-permute-done | bytes 131104 | tf_op jit(solution)/shard_map/ppermute | solution.py:26
  82.7 1.9 collective-permute-start.9
  84.6 5.0 %collective-permute-done.9 = bf16[512,128]{1,0:T(8,128)(2,1)S(1)} collective-permute-done((bf16[512,128]{1,0:T(8,128)(2,1)S(1)}, bf16[512,128]{1,0:T(8,128)(2,1)S(1)}, u32[]{:S(2)}, u32[]{:S(2)}) %collective-permute-start.9) | collective-permute-done | bytes 131104 | tf_op jit(solution)/shard_map/ppermute | solution.py:26
  89.6 1.9 collective-permute-start.10
  91.6 5.0 %collective-permute-done.10 = bf16[512,128]{1,0:T(8,128)(2,1)S(1)} collective-permute-done((bf16[512,128]{1,0:T(8,128)(2,1)S(1)}, bf16[512,128]{1,0:T(8,128)(2,1)S(1)}, u32[]{:S(2)}, u32[]{:S(2)}) %collective-permute-start.10) | collective-permute-done | bytes 131104 | tf_op jit(solution)/shard_map/ppermute | solution.py:26
  96.6 1.9 collective-permute-start.11
  98.5 5.1 %collective-permute-done.11 = bf16[512,128]{1,0:T(8,128)(2,1)S(1)} collective-permute-done((bf16[512,128]{1,0:T(8,128)(2,1)S(1)}, bf16[512,128]{1,0:T(8,128)(2,1)S(1)}, u32[]{:S(2)}, u32[]{:S(2)}) %collective-permute-start.11) | collective-permute-done | bytes 131104 | tf_op jit(solution)/shard_map/ppermute | solution.py:26
  103.6 1.9 collective-permute-start.12
  105.5 5.0 %collective-permute-done.12 = bf16[512,128]{1,0:T(8,128)(2,1)S(1)} collective-permute-done((bf16[512,128]{1,0:T(8,128)(2,1)S(1)}, bf16[512,128]{1,0:T(8,128)(2,1)S(1)}, u32[]{:S(2)}, u32[]{:S(2)}) %collective-permute-start.12) | collective-permute-done | bytes 131104 | tf_op jit(solution)/shard_map/ppermute | solution.py:26
  110.5 1.9 collective-permute-start.13
  112.4 5.0 %collective-permute-done.13 = bf16[512,128]{1,0:T(8,128)(2,1)S(1)} collective-permute-done((bf16[512,128]{1,0:T(8,128)(2,1)S(1)}, bf16[512,128]{1,0:T(8,128)(2,1)S(1)}, u32[]{:S(2)}, u32[]{:S(2)}) %collective-permute-start.13) | collective-permute-done | bytes 131104 | tf_op jit(solution)/shard_map/ppermute | solution.py:26
  117.4 1.9 collective-permute-start.14
  119.4 5.8 %collective-permute-done.14 = bf16[512,128]{1,0:T(8,128)(2,1)S(1)} collective-permute-done((bf16[512,128]{1,0:T(8,128)(2,1)S(1)}, bf16[512,128]{1,0:T(8,128)(2,1)S(1)}, u32[]{:S(2)}, u32[]{:S(2)}) %collective-permute-start.14) | collective-permute-done | bytes 131104 | tf_op jit(solution)/shard_map/ppermute | solution.py:26
  126.7 2.0 copy-done
  129.2 3.5 fusion.19
  132.7 4.9 %all-gather.10.cloned.1.call-done = bf16[384,2048]{1,0:T(8,128)(2,1)} async-done(((bf16[384,128]{1,0:T(8,128)(2,1)}), bf16[384,2048]{1,0:T(8,128)(2,1)}) %all-gather.10.cloned.1.call-update) | async-done | bytes 1572880 | tf_op jit(solution)/shard_map/all_gather | solution.py:44
  137.5 62.1 %all-gather.8.cloned.1.call-done = bf16[2048,384]{1,0:T(8,128)(2,1)} async-done(((bf16[128,384]{1,0:T(8,128)(2,1)}), bf16[2048,384]{1,0:T(8,128)(2,1)}) %all-gather.8.cloned.1.call-update) | async-done | bytes 1572880 | tf_op jit(solution)/shard_map/all_gather | solution.py:39
  199.6 7.0 %fusion.13 = f32[512,2048]{1,0:T(8,128)} fusion(bf16[384,2048]{1,0:T(8,128)(2,1)} %all-gather.10.cloned.1.call-done, f32[512,384]{1,0:T(8,128)S(1)} %fusion.19, bf16[2048,384]{1,0:T(8,128)(2,1)} %all-gather.8.cloned.1.call-done, f32[2048]{0:T(1024)S(1)} %copy-done.6, f32[512]{0:T(512)S(1)} %add_rsqrt_fusion.2, bf16[512,4096]{1,0:T(8,128)(2,1)} %copy-done, ...), kind=kOutput, calls=%fused_computation.22 | convolution fusion | flops 1615986688 | bytes 10233860 | tf_op jit(solution)/shard_map/dot_general | solution.py:42
  206.7 70.7 %reduce-scatter.2.cloned.1.call-done = f32[512,128]{1,0:T(8,128)} async-done(((f32[512,2048]{1,0:T(8,128)}), f32[512,128]{1,0:T(8,128)}) %reduce-scatter.2.cloned.1.call-update) | async-done | bytes 262160 | tf_op jit(solution)/shard_map/reduce_scatter | solution.py:47
  277.4 1.6 add_convert_fusion
  279.8 12.3 %collective-permute-start.15 = (bf16[512,128]{1,0:T(8,128)(2,1)}, bf16[512,128]{1,0:T(8,128)(2,1)S(1)}, u32[]{:S(2)}, u32[]{:S(2)}) collective-permute-start(bf16[512,128]{1,0:T(8,128)(2,1)} %add_convert_fusion), channel_id=1, source_target_pairs={{0,256},{256,0},{1,257},{257,1},{2,258},{258,2},{3,259},{259,3},{4... | collective-permute-start | bytes 393224 | tf_op jit(solution)/shard_map/ppermute | solution.py:13
  292.1 64.0 %all-gather.12.cloned.1.call-done = bf16[512,2048]{1,0:T(8,128)(2,1)} async-done(((bf16[512,128]{1,0:T(8,128)(2,1)}), bf16[512,2048]{1,0:T(8,128)(2,1)}) %all-gather.12.cloned.1.call-update) | async-done | bytes 2097168 | tf_op jit(solution)/shard_map/all_gather | solution.py:49
  356.1 2.1 fusion.3
  358.2 63.7 %all-gather.14.cloned.1.call-done = bf16[2048,256]{1,0:T(8,128)(2,1)} async-done(((bf16[128,256]{1,0:T(8,128)(2,1)}), bf16[2048,256]{1,0:T(8,128)(2,1)}) %all-gather.14.cloned.1.call-update) | async-done | bytes 1048592 | tf_op jit(solution)/shard_map/all_gather | solution.py:55
  421.9 2.8 bitcast_reduce_fusion
  424.9 4.0 collective-permute-start.16
  429.0 1.3 gather_fusion
  430.3 0.8 broadcast_select_fusion.1
  431.4 2.0 gather_fusion.1
  433.4 0.8 broadcast_select_fusion
  (74 shorter events, 3.9 us)
Async XLA Ops:
  7.2 118.7 %copy-start.1 = (bf16[512,128]{1,0:T(8,128)(2,1)S(1)}, bf16[512,128]{1,0:T(8,128)(2,1)}, u32[]{:S(2)}) copy-start(bf16[512,128]{1,0:T(8,128)(2,1)} %param.10) | copy-start | bytes 393220
  7.2 122.0 %all-gather.6.cloned.1.call-start = ((), (), s32[]{:S(2)}) async-start(), calls=%async_computation.1 | async-start | bytes 1671168 | tf_op jit(solution)/shard_map/all_gather | solution.py:35
  7.9 129.6 %all-gather.10.cloned.1.call-start = ((), (), s32[]{:S(2)}) async-start(), calls=%async_computation.3 | async-start | bytes 1671168 | tf_op jit(solution)/shard_map/all_gather | solution.py:44
  8.7 191.0 %all-gather.8.cloned.1.call-start = ((), (), s32[]{:S(2)}) async-start(), calls=%async_computation.2 | async-start | bytes 1671168 | tf_op jit(solution)/shard_map/all_gather | solution.py:39
  8.7 15.4 %collective-permute-start = (bf16[512,128]{1,0:T(8,128)(2,1)}, bf16[512,128]{1,0:T(8,128)(2,1)S(1)}, u32[]{:S(2)}, u32[]{:S(2)}) collective-permute-start(bf16[512,128]{1,0:T(8,128)(2,1)} %param.10), channel_id=1, source_target_pairs={{0,1},{1,2},{2,3},{3,4},{4,5},{5,6},{6,7},{7,8},{8,9},{9,10},{10,1... | collective-permute-start | bytes 393224 | tf_op jit(solution)/shard_map/ppermute | solution.py:26
  24.1 6.9 %collective-permute-start.1 = (bf16[512,128]{1,0:T(8,128)(2,1)S(1)}, bf16[512,128]{1,0:T(8,128)(2,1)S(1)}, u32[]{:S(2)}, u32[]{:S(2)}) collective-permute-start(bf16[512,128]{1,0:T(8,128)(2,1)S(1)} %collective-permute-done), channel_id=1, source_target_pairs={{0,1},{1,2},{2,3},{3,4},{4,5},{5,6},{6,7},{7,8},{8,9},{9,10},{10,1... | collective-permute-start | bytes 393224 | tf_op jit(solution)/shard_map/ppermute | solution.py:26
  31.0 6.9 %collective-permute-start.2 = (bf16[512,128]{1,0:T(8,128)(2,1)S(1)}, bf16[512,128]{1,0:T(8,128)(2,1)S(1)}, u32[]{:S(2)}, u32[]{:S(2)}) collective-permute-start(bf16[512,128]{1,0:T(8,128)(2,1)S(1)} %collective-permute-done.1), channel_id=1, source_target_pairs={{0,1},{1,2},{2,3},{3,4},{4,5},{5,6},{6,7},{7,8},{8,9},{9,10},{10,1... | collective-permute-start | bytes 393224 | tf_op jit(solution)/shard_map/ppermute | solution.py:26
  37.9 6.9 %collective-permute-start.3 = (bf16[512,128]{1,0:T(8,128)(2,1)S(1)}, bf16[512,128]{1,0:T(8,128)(2,1)S(1)}, u32[]{:S(2)}, u32[]{:S(2)}) collective-permute-start(bf16[512,128]{1,0:T(8,128)(2,1)S(1)} %collective-permute-done.2), channel_id=1, source_target_pairs={{0,1},{1,2},{2,3},{3,4},{4,5},{5,6},{6,7},{7,8},{8,9},{9,10},{10,1... | collective-permute-start | bytes 393224 | tf_op jit(solution)/shard_map/ppermute | solution.py:26
  44.8 6.9 %collective-permute-start.4 = (bf16[512,128]{1,0:T(8,128)(2,1)S(1)}, bf16[512,128]{1,0:T(8,128)(2,1)S(1)}, u32[]{:S(2)}, u32[]{:S(2)}) collective-permute-start(bf16[512,128]{1,0:T(8,128)(2,1)S(1)} %collective-permute-done.3), channel_id=1, source_target_pairs={{0,1},{1,2},{2,3},{3,4},{4,5},{5,6},{6,7},{7,8},{8,9},{9,10},{10,1... | collective-permute-start | bytes 393224 | tf_op jit(solution)/shard_map/ppermute | solution.py:26
  51.7 6.9 %collective-permute-start.5 = (bf16[512,128]{1,0:T(8,128)(2,1)S(1)}, bf16[512,128]{1,0:T(8,128)(2,1)S(1)}, u32[]{:S(2)}, u32[]{:S(2)}) collective-permute-start(bf16[512,128]{1,0:T(8,128)(2,1)S(1)} %collective-permute-done.4), channel_id=1, source_target_pairs={{0,1},{1,2},{2,3},{3,4},{4,5},{5,6},{6,7},{7,8},{8,9},{9,10},{10,1... | collective-permute-start | bytes 393224 | tf_op jit(solution)/shard_map/ppermute | solution.py:26
  58.6 8.1 %collective-permute-start.6 = (bf16[512,128]{1,0:T(8,128)(2,1)S(1)}, bf16[512,128]{1,0:T(8,128)(2,1)S(1)}, u32[]{:S(2)}, u32[]{:S(2)}) collective-permute-start(bf16[512,128]{1,0:T(8,128)(2,1)S(1)} %collective-permute-done.5), channel_id=1, source_target_pairs={{0,1},{1,2},{2,3},{3,4},{4,5},{5,6},{6,7},{7,8},{8,9},{9,10},{10,1... | collective-permute-start | bytes 393224 | tf_op jit(solution)/shard_map/ppermute | solution.py:26
  66.7 8.4 %collective-permute-start.7 = (bf16[512,128]{1,0:T(8,128)(2,1)S(1)}, bf16[512,128]{1,0:T(8,128)(2,1)S(1)}, u32[]{:S(2)}, u32[]{:S(2)}) collective-permute-start(bf16[512,128]{1,0:T(8,128)(2,1)S(1)} %collective-permute-done.6), channel_id=1, source_target_pairs={{0,1},{1,2},{2,3},{3,4},{4,5},{5,6},{6,7},{7,8},{8,9},{9,10},{10,1... | collective-permute-start | bytes 393224 | tf_op jit(solution)/shard_map/ppermute | solution.py:26
  75.2 7.6 %collective-permute-start.8 = (bf16[512,128]{1,0:T(8,128)(2,1)S(1)}, bf16[512,128]{1,0:T(8,128)(2,1)S(1)}, u32[]{:S(2)}, u32[]{:S(2)}) collective-permute-start(bf16[512,128]{1,0:T(8,128)(2,1)S(1)} %collective-permute-done.7), channel_id=1, source_target_pairs={{0,1},{1,2},{2,3},{3,4},{4,5},{5,6},{6,7},{7,8},{8,9},{9,10},{10,1... | collective-permute-start | bytes 393224 | tf_op jit(solution)/shard_map/ppermute | solution.py:26
  82.7 6.9 %collective-permute-start.9 = (bf16[512,128]{1,0:T(8,128)(2,1)S(1)}, bf16[512,128]{1,0:T(8,128)(2,1)S(1)}, u32[]{:S(2)}, u32[]{:S(2)}) collective-permute-start(bf16[512,128]{1,0:T(8,128)(2,1)S(1)} %collective-permute-done.8), channel_id=1, source_target_pairs={{0,1},{1,2},{2,3},{3,4},{4,5},{5,6},{6,7},{7,8},{8,9},{9,10},{10,1... | collective-permute-start | bytes 393224 | tf_op jit(solution)/shard_map/ppermute | solution.py:26
  89.6 6.9 %collective-permute-start.10 = (bf16[512,128]{1,0:T(8,128)(2,1)S(1)}, bf16[512,128]{1,0:T(8,128)(2,1)S(1)}, u32[]{:S(2)}, u32[]{:S(2)}) collective-permute-start(bf16[512,128]{1,0:T(8,128)(2,1)S(1)} %collective-permute-done.9), channel_id=1, source_target_pairs={{0,1},{1,2},{2,3},{3,4},{4,5},{5,6},{6,7},{7,8},{8,9},{9,10},{10,1... | collective-permute-start | bytes 393224 | tf_op jit(solution)/shard_map/ppermute | solution.py:26
  96.6 7.0 %collective-permute-start.11 = (bf16[512,128]{1,0:T(8,128)(2,1)S(1)}, bf16[512,128]{1,0:T(8,128)(2,1)S(1)}, u32[]{:S(2)}, u32[]{:S(2)}) collective-permute-start(bf16[512,128]{1,0:T(8,128)(2,1)S(1)} %collective-permute-done.10), channel_id=1, source_target_pairs={{0,1},{1,2},{2,3},{3,4},{4,5},{5,6},{6,7},{7,8},{8,9},{9,10},{10,1... | collective-permute-start | bytes 393224 | tf_op jit(solution)/shard_map/ppermute | solution.py:26
  103.6 6.9 %collective-permute-start.12 = (bf16[512,128]{1,0:T(8,128)(2,1)S(1)}, bf16[512,128]{1,0:T(8,128)(2,1)S(1)}, u32[]{:S(2)}, u32[]{:S(2)}) collective-permute-start(bf16[512,128]{1,0:T(8,128)(2,1)S(1)} %collective-permute-done.11), channel_id=1, source_target_pairs={{0,1},{1,2},{2,3},{3,4},{4,5},{5,6},{6,7},{7,8},{8,9},{9,10},{10,1... | collective-permute-start | bytes 393224 | tf_op jit(solution)/shard_map/ppermute | solution.py:26
  110.5 6.9 %collective-permute-start.13 = (bf16[512,128]{1,0:T(8,128)(2,1)S(1)}, bf16[512,128]{1,0:T(8,128)(2,1)S(1)}, u32[]{:S(2)}, u32[]{:S(2)}) collective-permute-start(bf16[512,128]{1,0:T(8,128)(2,1)S(1)} %collective-permute-done.12), channel_id=1, source_target_pairs={{0,1},{1,2},{2,3},{3,4},{4,5},{5,6},{6,7},{7,8},{8,9},{9,10},{10,1... | collective-permute-start | bytes 393224 | tf_op jit(solution)/shard_map/ppermute | solution.py:26
  117.4 7.8 %collective-permute-start.14 = (bf16[512,128]{1,0:T(8,128)(2,1)S(1)}, bf16[512,128]{1,0:T(8,128)(2,1)S(1)}, u32[]{:S(2)}, u32[]{:S(2)}) collective-permute-start(bf16[512,128]{1,0:T(8,128)(2,1)S(1)} %collective-permute-done.13), channel_id=1, source_target_pairs={{0,1},{1,2},{2,3},{3,4},{4,5},{5,6},{6,7},{7,8},{8,9},{9,10},{10,1... | collective-permute-start | bytes 393224 | tf_op jit(solution)/shard_map/ppermute | solution.py:26
  119.3 158.0 %reduce-scatter.2.cloned.1.call-start = ((), (), s32[]{:S(2)}) async-start(), calls=%async_computation.4 | async-start | bytes 4456448 | tf_op jit(solution)/shard_map/reduce_scatter | solution.py:47
  125.5 3.6 copy-start.6
  126.7 2.0 copy-start
  206.6 73.0 %copy-start.3 = (s32[512]{0:T(512)S(1)}, s32[512]{0:T(512)}, u32[]{:S(2)}) copy-start(s32[512]{0:T(512)} %param.19) | copy-start | bytes 6148
  206.6 73.2 %copy-start.4 = (f32[128]{0:T(128)S(1)}, f32[128]{0:T(128)}, u32[]{:S(2)}) copy-start(f32[128]{0:T(128)} %param.18) | copy-start | bytes 1540
  206.6 73.2 %copy-start.5 = (f32[128]{0:T(128)S(1)}, f32[128]{0:T(128)}, u32[]{:S(2)}) copy-start(f32[128]{0:T(128)} %param.17) | copy-start | bytes 1540
  206.6 215.3 %copy-start.7 = (f32[2048]{0:T(1024)S(1)}, f32[2048]{0:T(1024)}, u32[]{:S(2)}) copy-start(f32[2048]{0:T(1024)} %param.15) | copy-start | bytes 24580
  206.6 149.5 %all-gather.12.cloned.1.call-start = ((), (), s32[]{:S(2)}) async-start(), calls=%async_computation.5 | async-start | bytes 2228224 | tf_op jit(solution)/shard_map/all_gather | solution.py:49
  279.0 142.9 %all-gather.14.cloned.1.call-start = ((), (), s32[]{:S(2)}) async-start(), calls=%async_computation.6 | async-start | bytes 1114112 | tf_op jit(solution)/shard_map/all_gather | solution.py:55
  279.8 149.1 %copy-start.2 = (bf16[512,128]{1,0:T(8,128)(2,1)S(1)}, bf16[512,128]{1,0:T(8,128)(2,1)}, u32[]{:S(2)}) copy-start(bf16[512,128]{1,0:T(8,128)(2,1)} %add_convert_fusion) | copy-start | bytes 393220
  279.8 149.1 %collective-permute-start.15 = (bf16[512,128]{1,0:T(8,128)(2,1)}, bf16[512,128]{1,0:T(8,128)(2,1)S(1)}, u32[]{:S(2)}, u32[]{:S(2)}) collective-permute-start(bf16[512,128]{1,0:T(8,128)(2,1)} %add_convert_fusion), channel_id=1, source_target_pairs={{0,256},{256,0},{1,257},{257,1},{2,258},{258,2},{3,259},{259,3},{4... | collective-permute-start | bytes 393224 | tf_op jit(solution)/shard_map/ppermute | solution.py:13
  424.9 6.2 %collective-permute-start.16 = (bf16[512,256]{0,1:T(8,128)(2,1)S(1)}, bf16[512,256]{0,1:T(8,128)(2,1)S(1)}, u32[]{:S(2)}, u32[]{:S(2)}) collective-permute-start(bf16[512,256]{0,1:T(8,128)(2,1)S(1)} %fusion.12), channel_id=1, source_target_pairs={{0,256},{256,0},{1,257},{257,1},{2,258},{258,2},{3,259},{259,3},{4... | collective-permute-start | bytes 786440 | tf_op jit(solution)/shard_map/ppermute | solution.py:13
Sparse Core Ops, SparseCore 0:
  11.0 63.5 all-gather.5
  77.6 59.8 all-gather.9
  140.5 59.0 all-gather.7
  206.7 70.5 reduce-scatter.1
  279.8 76.3 all-gather.11
  359.0 62.8 all-gather.13
